TPU v7x, 32 devices: a whole 2x2x4 slice. The times are simulated.
32 devices in a mesh: tbl: 8 (over z, core), grp: 4 (over y, x).
Axes of the slice: x: 2, y: 2, z: 4, core: 2. Of those that a mesh axis runs over, the one named last changes fastest.
Arguments:
- codes: bfloat16 [8, 1024, 256], P('tbl', 'grp'), may hold values from -4 to 4
- row_scales: float32 [8, 1024], P('tbl', 'grp'), may hold values from 0.25 to 16
- history_lengths: int32 [32, 8], P(None, 'tbl'), may hold values from 1 to 32, as said below
- history_ids: int32 [32, 8, 32], P(None, 'tbl'), may hold values from 0 to 1023, as said below
- query_items: int32 [32, 8], P(None, 'tbl'), may hold values from 0 to 1023, as said below
- slot_tables: int32 [8], replicated, may hold values from 0 to 7, each once
Outputs:
- pooled: bfloat16 [32, 8, 256], P(('tbl', 'grp'))
Inputs may be any that keep to these rules, and one draw needn't show every extreme that they name: `history_lengths`: the largest length, 32, occurs in every draw. `history_ids`: entries at positions at or beyond the history's length are row ids too, and are to be ignored. query_items[b, s] equals history_ids[b, s, h] for some h below history_lengths[b, s].
All inputs are finite; a program needn't handle non-finite values.
Results may differ from a plain program's by a relative error of at most 0.004.
Values may be sent and summed in bfloat16 or wider, within the bound.
A program may use at most 64 MiB of HBM per device.

v0:
```python
import jax
import jax.numpy as jnp
from jax import lax
from jax.sharding import PartitionSpec as P


def combined_all(value, axis, combine):
    everything = jax.tree.map(lambda part: lax.all_gather(part, axis), value)
    leading = jax.tree.map(lambda part: part[0], everything)

    def hop(k, so_far):
        return combine(so_far, jax.tree.map(lambda part: part[k], everything))

    return lax.fori_loop(1, lax.axis_size(axis), hop, leading)


def combine(first, second):
    first_peak, first_mass, first_sums = first
    second_peak, second_mass, second_sums = second
    peak = jnp.maximum(first_peak, second_peak)
    first_factor = jnp.exp(first_peak - peak)
    second_factor = jnp.exp(second_peak - peak)
    return (
        peak,
        first_mass * first_factor + second_mass * second_factor,
        first_sums * first_factor[..., None] + second_sums * second_factor[..., None],
    )


def per_device(codes, row_scales, history_lengths, history_ids, query_items, slot_tables):
    slot_count, row_count, emb_width = codes.shape
    batch_rows, _, history = history_ids.shape
    tbl_count = lax.axis_size("tbl")
    grp_count = lax.axis_size("grp")
    owned_rows = batch_rows // (tbl_count * grp_count)
    grp_index = lax.axis_index("grp")
    offset = grp_index * row_count
    query_local = query_items - offset
    query_owned = (query_local >= 0) & (query_local < row_count)
    query_index = jnp.clip(query_local, 0, row_count - 1)
    found = jnp.take(codes[0], query_index[:, 0], axis=0).astype(jnp.float32)
    factor = jnp.take(row_scales[0], query_index[:, 0], axis=0)
    code_parts = [jnp.where(query_owned[:, 0, None], found, 0.0)]
    scale_parts = [jnp.where(query_owned[:, 0], factor, 0.0)]
    query_codes = jnp.stack(code_parts, axis=1)
    query_scales = jnp.stack(scale_parts, axis=1)
    query = lax.psum((query_codes * query_scales[..., None]).astype(jnp.bfloat16), "grp").astype(
        jnp.float32
    )
    positions = jnp.arange(history, dtype=jnp.int32)
    row_iota = jnp.arange(row_count, dtype=jnp.int32)
    table_rows = codes.astype(jnp.float32)
    block_count = 8
    block_rows = batch_rows // block_count

    def partial_value(block):
        block_ids, block_lengths, block_query = block
        local = block_ids - offset
        live = positions[None, None, :] < block_lengths[:, :, None]
        local = jnp.where(live, local, -1)
        peaks, masses, sums = ([], [], [])
        rows_f = table_rows[0]
        factor = row_scales[0]
        counts = jnp.sum(
            (local[:, 0, :, None] == row_iota[None, None, :]).astype(jnp.float32), axis=1
        )
        raw = jnp.dot(block_query[:, 0], rows_f.T, precision=lax.Precision.HIGHEST)
        score = raw * factor[None, :] / emb_width
        named = counts > 0.0
        peak = jnp.max(jnp.where(named, score, -1e30), axis=1)
        weight = jnp.where(
            named,
            counts * jnp.exp(jnp.where(named, score, 0.0) - jnp.where(named, peak[:, None], 0.0)),
            0.0,
        )
        peaks.append(peak)
        masses.append(jnp.sum(weight, axis=1))
        sums.append(jnp.dot(weight * factor[None, :], rows_f, precision=lax.Precision.HIGHEST))
        return (jnp.stack(peaks, axis=1), jnp.stack(masses, axis=1), jnp.stack(sums, axis=1))

    block_peaks, block_masses, block_sums = lax.map(
        partial_value,
        (
            history_ids.reshape(block_count, block_rows, slot_count, history),
            history_lengths.reshape(block_count, block_rows, slot_count),
            query.reshape(block_count, block_rows, slot_count, emb_width),
        ),
    )
    lead = (tbl_count, grp_count, owned_rows)
    peaks = block_peaks.reshape(lead + (slot_count,))
    masses = block_masses.reshape(lead + (slot_count,))
    sums = block_sums.reshape(lead + (slot_count, emb_width))
    all_peak, all_mass, all_sums = combined_all((peaks, masses, sums), "grp", combine)
    mass = lax.dynamic_index_in_dim(all_mass, grp_index, 1, keepdims=False)
    weighted = lax.dynamic_index_in_dim(all_sums, grp_index, 1, keepdims=False)
    pooled_slot = (weighted / mass[..., None]).astype(jnp.bfloat16)
    outgoing = jnp.transpose(pooled_slot, (1, 0, 2, 3))
    arrived = lax.all_to_all(outgoing, "tbl", split_axis=1, concat_axis=1, tiled=True)
    arranged = arrived.reshape(owned_rows, tbl_count * slot_count, emb_width)
    inverse = jnp.argsort(slot_tables)
    return jnp.take(arranged, inverse, axis=1)


def solution(mesh):
    placed = (
        P("tbl", "grp", None),
        P("tbl", "grp"),
        P(None, "tbl"),
        P(None, "tbl", None),
        P(None, "tbl"),
        P(),
    )
    return jax.shard_map(
        per_device,
        mesh=mesh,
        in_specs=placed,
        out_specs=P(("tbl", "grp"), None, None),
        check_vma=False,
    )
```

profile of v0, /device:TPU:0, one launch (start us, length us, event | category | flops | bytes accessed | tf_op | source)
XLA Modules:
  0.0 74.8 jit_solution(50232354431573683)
XLA Ops:
  0.0 0.7 copy-done.2
  0.7 0.7 copy-done
  1.4 0.7 gather_fusion.1
  3.0 17.8 %psum.7 = bf16[8,4,1,256]{3,2,1,0:T(2,128)(2,1)S(1)} all-reduce(bf16[8,4,1,256]{3,2,1,0:T(2,128)(2,1)S(1)} %reshape.329), channel_id=1, replica_groups=mesh['tbl'=8,'grp'=4] {'grp'}, use_global_device_ids=true, to_apply=%region_1.2 | all-reduce | flops 8192 | bytes 32768 | tf_op jit(solution)/shard_map/psum | solution.py:47
  21.5 0.7 reduce.3
  22.3 14.2 %while.35 = (s32[]{:T(128)}, f32[8,4,1]{1,2,0:T(1,128)S(1)}, f32[8,4,1]{1,2,0:T(1,128)S(1)}, f32[8,4,1,256]{3,1,2,0:T(4,128)S(1)}, s32[8,4,1]{1,2,0:T(1,128)S(1)...) while((s32[]{:T(128)}, f32[8,4,1]{1,2,0:T(1,128)S(1)}, ...), condition=%wide.region_6.7_spmd.clone, body=%wide.region_2.6_spmd.clone.sunk | while | flops 6402426 | bytes 575205 | solution.py:81
  22.3 0.8 %bitcast_select_fusion.4 = s32[4,32]{1,0:T(4,128)S(1)} fusion(s32[8,4,1,32]{3,1,2,0:T(4,128)} %get-tuple-element.560, s32[]{:T(128)} %get-tuple-element.544, s32[]{:T(128)} %get-tuple-element.561, s32[4]{0:T(128)S(1)} %fusion.37), kind=kLoop, calls=%fused_computation.31.clone.1 | loop fusion | flops 384 | bytes 1048 | tf_op jit(solution)/shard_map/while/body/eval_jaxpr/jit(_where)/select_n | solution.py:60
  24.0 0.8 %bitcast_select_fusion.4 = s32[4,32]{1,0:T(4,128)S(1)} fusion(s32[8,4,1,32]{3,1,2,0:T(4,128)} %get-tuple-element.560, s32[]{:T(128)} %get-tuple-element.544, s32[]{:T(128)} %get-tuple-element.561, s32[4]{0:T(128)S(1)} %fusion.37), kind=kLoop, calls=%fused_computation.31.clone.1 | loop fusion | flops 384 | bytes 1048 | tf_op jit(solution)/shard_map/while/body/eval_jaxpr/jit(_where)/select_n | solution.py:60
  25.8 0.8 %bitcast_select_fusion.4 = s32[4,32]{1,0:T(4,128)S(1)} fusion(s32[8,4,1,32]{3,1,2,0:T(4,128)} %get-tuple-element.560, s32[]{:T(128)} %get-tuple-element.544, s32[]{:T(128)} %get-tuple-element.561, s32[4]{0:T(128)S(1)} %fusion.37), kind=kLoop, calls=%fused_computation.31.clone.1 | loop fusion | flops 384 | bytes 1048 | tf_op jit(solution)/shard_map/while/body/eval_jaxpr/jit(_where)/select_n | solution.py:60
  27.6 0.8 %bitcast_select_fusion.4 = s32[4,32]{1,0:T(4,128)S(1)} fusion(s32[8,4,1,32]{3,1,2,0:T(4,128)} %get-tuple-element.560, s32[]{:T(128)} %get-tuple-element.544, s32[]{:T(128)} %get-tuple-element.561, s32[4]{0:T(128)S(1)} %fusion.37), kind=kLoop, calls=%fused_computation.31.clone.1 | loop fusion | flops 384 | bytes 1048 | tf_op jit(solution)/shard_map/while/body/eval_jaxpr/jit(_where)/select_n | solution.py:60
  29.4 0.8 %bitcast_select_fusion.4 = s32[4,32]{1,0:T(4,128)S(1)} fusion(s32[8,4,1,32]{3,1,2,0:T(4,128)} %get-tuple-element.560, s32[]{:T(128)} %get-tuple-element.544, s32[]{:T(128)} %get-tuple-element.561, s32[4]{0:T(128)S(1)} %fusion.37), kind=kLoop, calls=%fused_computation.31.clone.1 | loop fusion | flops 384 | bytes 1048 | tf_op jit(solution)/shard_map/while/body/eval_jaxpr/jit(_where)/select_n | solution.py:60
  31.2 0.8 %bitcast_select_fusion.4 = s32[4,32]{1,0:T(4,128)S(1)} fusion(s32[8,4,1,32]{3,1,2,0:T(4,128)} %get-tuple-element.560, s32[]{:T(128)} %get-tuple-element.544, s32[]{:T(128)} %get-tuple-element.561, s32[4]{0:T(128)S(1)} %fusion.37), kind=kLoop, calls=%fused_computation.31.clone.1 | loop fusion | flops 384 | bytes 1048 | tf_op jit(solution)/shard_map/while/body/eval_jaxpr/jit(_where)/select_n | solution.py:60
  33.0 0.8 %bitcast_select_fusion.4 = s32[4,32]{1,0:T(4,128)S(1)} fusion(s32[8,4,1,32]{3,1,2,0:T(4,128)} %get-tuple-element.560, s32[]{:T(128)} %get-tuple-element.544, s32[]{:T(128)} %get-tuple-element.561, s32[4]{0:T(128)S(1)} %fusion.37), kind=kLoop, calls=%fused_computation.31.clone.1 | loop fusion | flops 384 | bytes 1048 | tf_op jit(solution)/shard_map/while/body/eval_jaxpr/jit(_where)/select_n | solution.py:60
  34.7 0.8 %bitcast_select_fusion.4 = s32[4,32]{1,0:T(4,128)S(1)} fusion(s32[8,4,1,32]{3,1,2,0:T(4,128)} %get-tuple-element.560, s32[]{:T(128)} %get-tuple-element.544, s32[]{:T(128)} %get-tuple-element.561, s32[4]{0:T(128)S(1)} %fusion.37), kind=kLoop, calls=%fused_computation.31.clone.1 | loop fusion | flops 384 | bytes 1048 | tf_op jit(solution)/shard_map/while/body/eval_jaxpr/jit(_where)/select_n | solution.py:60
  36.5 7.5 %all-gather.2 = f32[32,4,1,256]{3,1,2,0:T(4,128)S(1)} all-gather(f32[8,4,1,256]{3,1,2,0:T(4,128)S(1)} %get-tuple-element.250), channel_id=4, replica_groups=mesh['tbl'=8,'grp'=4] {'grp'}, dimensions={0}, use_global_device_ids=true | all-gather | bytes 163840 | tf_op jit(solution)/shard_map/all_gather | solution.py:8
  44.1 8.1 %all-gather = f32[32,4,1]{1,2,0:T(1,128)S(1)} all-gather(f32[8,4,1]{1,2,0:T(1,128)S(1)} %get-tuple-element.248), channel_id=2, replica_groups=mesh['tbl'=8,'grp'=4] {'grp'}, dimensions={0}, use_global_device_ids=true | all-gather | bytes 640 | tf_op jit(solution)/shard_map/all_gather | solution.py:8
  52.3 7.3 %all-gather.1 = f32[32,4,1]{1,2,0:T(1,128)S(1)} all-gather(f32[8,4,1]{1,2,0:T(1,128)S(1)} %get-tuple-element.249), channel_id=3, replica_groups=mesh['tbl'=8,'grp'=4] {'grp'}, dimensions={0}, use_global_device_ids=true | all-gather | bytes 640 | tf_op jit(solution)/shard_map/all_gather | solution.py:8
  59.8 1.4 %while.34 = (s32[]{:T(128)}, f32[8,4,1,1]{0,1,3,2:T(4,128)S(1)}, f32[8,4,1,1]{0,1,3,2:T(4,128)S(1)}, f32[8,4,1,1,256]{4,3,2,1,0:T(1,128)S(1)}, f32[4,8,4,1,1]{1,...) while((s32[]{:T(128)}, f32[8,4,1,1]{0,1,3,2:T(4,128)S(1)}, ...), condition=%wide.region_8.9_spmd, body=%wide.region_7.8_spmd.sunk | while | flops 24805 | bytes 166427 | solution.py:14
  61.9 0.7 reduce.4
  63.1 4.9 %all-to-all-start = ((bf16[8,2,128]{2,1,0:T(2,128)(2,1)}), bf16[8,2,128]{2,1,0:T(2,128)(2,1)S(1)}, u32[]{:S(2)}, u32[]{:S(2)}) async-start(bf16[8,2,128]{2,1,0:T(2,128)(2,1)} %reshape.339), calls=%async_computation | async-start | bytes 8192 | tf_op jit(solution)/shard_map/all_to_all | solution.py:98
  68.0 0.6 copy-done.4
  68.7 1.0 %sort.17 = (s32[8]{0:T(128)}, s32[8]{0:T(128)S(1)}) sort(s32[8]{0:T(128)S(1)} %copy-done.4, s32[8]{0:T(128)S(1)} %iota.10), dimensions={0}, to_apply=%region_0.1 | sort | flops 24 | bytes 128 | tf_op jit(solution)/shard_map/jit(argsort)/sort | solution.py:100
  69.7 3.8 %all-to-all-done = bf16[8,2,128]{2,1,0:T(2,128)(2,1)S(1)} async-done(((bf16[8,2,128]{2,1,0:T(2,128)(2,1)}), bf16[8,2,128]{2,1,0:T(2,128)(2,1)S(1)}, u32[]{:S(2)}, u32[]{:S(2)}) %all-to-all-start) | async-done | bytes 4128 | tf_op jit(solution)/shard_map/all_to_all | solution.py:98
  74.1 0.7 bitcast_select_fusion.2
  (116 shorter events, 13.1 us)
Async XLA Ops:
  0.0 0.7 copy-start.2
  0.7 0.7 copy-start
  1.4 0.9 %copy-start.1 = (bf16[1,256,256]{2,1,0:T(8,128)(2,1)S(1)}, bf16[1,256,256]{2,1,0:T(8,128)(2,1)}, u32[]{:S(2)}) copy-start(bf16[1,256,256]{2,1,0:T(8,128)(2,1)} %param.10) | copy-start | bytes 393220
  20.9 0.7 copy-start.3
  63.1 10.4 %all-to-all-start = ((bf16[8,2,128]{2,1,0:T(2,128)(2,1)}), bf16[8,2,128]{2,1,0:T(2,128)(2,1)S(1)}, u32[]{:S(2)}, u32[]{:S(2)}) async-start(bf16[8,2,128]{2,1,0:T(2,128)(2,1)} %reshape.339), calls=%async_computation | async-start | bytes 8192 | tf_op jit(solution)/shard_map/all_to_all | solution.py:98
  68.0 0.7 copy-start.4
where the time goes:
time: 75.3 us; the launch traced here: 74.8 us
  blocking collectives  40.7 us (54%)
  other arithmetic  12.5 us (17%)
  local copies, waits for them, and re-layouts  7.25 us (10%)
  matrix products  5.05 us (7%)
  starting transfers between devices  4.88 us (6%)
  waiting for transfers between devices  3.79 us (5%)
    all_gather x3, blocking collectives, combined_all(): everything = jax.tree.map(lambda part: lax.all_gather(part, axis), value)  22.9 us
    psum x1, blocking collectives, per_device(): lax.psum((query_codes * query_scales[..., None]).astype(jnp.bfloat16), 'g...  17.8 us
    select_n x8, other arithmetic, partial_value(): local = jnp.where(live, local, -1)  6.06 us
    all_to_all x1, starting transfers between devices, per_device(): lax.all_to_all(outgoing, 'tbl', split_axis=1, concat_axis=1, tiled=True)  4.88 us
    unnamed x15, local copies, waits for them, and re-layouts  3.95 us
    all_to_all x1, waiting for transfers between devices, per_device(): lax.all_to_all(outgoing, 'tbl', split_axis=1, concat_axis=1, tiled=True)  3.79 us
    dot_general x8, matrix products, partial_value(): raw = jnp.dot(block_query[:, 0], rows_f.T, precision=lax.Precision.HIGHEST)  3.42 us
    dot_general x8, matrix products, partial_value(): jnp.dot(weight * factor[None, :], rows_f, precision=lax.Precision.HIGHEST)  1.63 us
  transfers between devices with their start and end apart: 1, of which 1 were waited for; matrix products, arithmetic and copies ran while one was open for 1% of the time, Pallas kernels for 0%

commit v1 on v0

--- a/solution.py
+++ b/solution.py
@@ -44,9 +44,9 @@
     scale_parts = [jnp.where(query_owned[:, 0], factor, 0.0)]
     query_codes = jnp.stack(code_parts, axis=1)
     query_scales = jnp.stack(scale_parts, axis=1)
-    query = lax.psum((query_codes * query_scales[..., None]).astype(jnp.bfloat16), "grp").astype(
-        jnp.float32
-    )
+    query = jnp.sum(
+        lax.all_gather((query_codes * query_scales[..., None]).astype(jnp.bfloat16), "grp"), axis=0
+    ).astype(jnp.float32)
     positions = jnp.arange(history, dtype=jnp.int32)
     row_iota = jnp.arange(row_count, dtype=jnp.int32)
     table_rows = codes.astype(jnp.float32)

time: 75.3 us -> 68.2 us (0.906)
  blocking collectives: 40.7 us -> 33.6 us
    psum x1 -> x0, blocking collectives: 17.8 us -> none  [per_device(): lax.psum((query_codes * query_scales[..., None]).astype(jnp.bfloat16), 'g...]
    all_gather x0 -> x1, blocking collectives: none -> 9.72 us  [per_device(): lax.all_gather((query_codes * query_scales[..., None]).astype(jnp.bfloat1...]
    all_gather x3, blocking collectives: 22.9 us -> 23.8 us  [combined_all(): everything = jax.tree.map(lambda part: lax.all_gather(part, axis), value)]
  transfers between devices with their start and end apart: 1 -> 1, of which waited for: 1 -> 1; matrix products, arithmetic and copies ran while one was open for 1% -> 2% of each run, Pallas kernels for 0% -> 0%
where the time goes in v1:
time: 68.2 us; the launch traced here: 67.7 us
  blocking collectives  33.6 us (49%)
  other arithmetic  12.5 us (18%)
  local copies, waits for them, and re-layouts  7.28 us (11%)
  matrix products  5.05 us (7%)
  starting transfers between devices  4.88 us (7%)
  waiting for transfers between devices  3.79 us (6%)
    all_gather x3, blocking collectives, combined_all(): everything = jax.tree.map(lambda part: lax.all_gather(part, axis), value)  23.8 us
    all_gather x1, blocking collectives, per_device(): lax.all_gather((query_codes * query_scales[..., None]).astype(jnp.bfloat1...  9.72 us
    select_n x8, other arithmetic, partial_value(): local = jnp.where(live, local, -1)  6.06 us
    all_to_all x1, starting transfers between devices, per_device(): lax.all_to_all(outgoing, 'tbl', split_axis=1, concat_axis=1, tiled=True)  4.88 us
    unnamed x15, local copies, waits for them, and re-layouts  3.95 us
    all_to_all x1, waiting for transfers between devices, per_device(): lax.all_to_all(outgoing, 'tbl', split_axis=1, concat_axis=1, tiled=True)  3.79 us
    dot_general x8, matrix products, partial_value(): raw = jnp.dot(block_query[:, 0], rows_f.T, precision=lax.Precision.HIGHEST)  3.42 us
    dot_general x8, matrix products, partial_value(): jnp.dot(weight * factor[None, :], rows_f, precision=lax.Precision.HIGHEST)  1.63 us
  transfers between devices with their start and end apart: 1, of which 1 were waited for; matrix products, arithmetic and copies ran while one was open for 2% of the time, Pallas kernels for 0%

profile of v1, /device:TPU:0, one launch (start us, length us, event | category | flops | bytes accessed | tf_op | source)
XLA Modules:
  0.0 67.7 jit_solution(5976676111412366025)
XLA Ops:
  0.0 0.7 copy-done.2
  0.7 0.7 copy-done
  1.4 0.7 %gather_fusion.1 = f32[32]{0:T(128)S(1)} fusion(f32[256]{0:T(256)S(1)} %bitcast.113, s32[1024]{0:T(1024)S(1)} %pad_clamp_fusion.1), kind=kCustom, calls=%fused_computation.1 | custom fusion | bytes 384 | tf_op jit(solution)/shard_map/jit(_take)/gather | solution.py:42
  3.0 9.7 %all_gather.13 = bf16[4,32,1,256]{3,1,2,0:T(8,128)(2,1)S(1)} all-gather(bf16[1,32,1,256]{3,1,2,0:T(8,128)(2,1)S(1)} %multiply_convert_fusion), channel_id=1, replica_groups=mesh['tbl'=8,'grp'=4] {'grp'}, dimensions={0}, use_global_device_ids=true | all-gather | bytes 81920 | tf_op jit(solution)/shard_map/all_gather | solution.py:48
  13.5 0.7 reduce.5
  14.2 14.2 %while.35 = (s32[]{:T(128)}, f32[8,4,1]{1,2,0:T(1,128)S(1)}, f32[8,4,1]{1,2,0:T(1,128)S(1)}, f32[8,4,1,256]{3,1,2,0:T(4,128)S(1)}, s32[8,4,1]{1,2,0:T(1,128)S(1)...) while((s32[]{:T(128)}, f32[8,4,1]{1,2,0:T(1,128)S(1)}, ...), condition=%wide.region_6.7_spmd.clone, body=%wide.region_2.6_spmd.clone.sunk | while | flops 6402426 | bytes 575205 | solution.py:81
  14.2 0.8 %bitcast_select_fusion.4 = s32[4,32]{1,0:T(4,128)S(1)} fusion(s32[8,4,1,32]{3,1,2,0:T(4,128)} %get-tuple-element.560, s32[]{:T(128)} %get-tuple-element.544, s32[]{:T(128)} %get-tuple-element.561, s32[4]{0:T(128)S(1)} %fusion.37), kind=kLoop, calls=%fused_computation.31.clone.1 | loop fusion | flops 384 | bytes 1048 | tf_op jit(solution)/shard_map/while/body/eval_jaxpr/jit(_where)/select_n | solution.py:60
  16.0 0.8 %bitcast_select_fusion.4 = s32[4,32]{1,0:T(4,128)S(1)} fusion(s32[8,4,1,32]{3,1,2,0:T(4,128)} %get-tuple-element.560, s32[]{:T(128)} %get-tuple-element.544, s32[]{:T(128)} %get-tuple-element.561, s32[4]{0:T(128)S(1)} %fusion.37), kind=kLoop, calls=%fused_computation.31.clone.1 | loop fusion | flops 384 | bytes 1048 | tf_op jit(solution)/shard_map/while/body/eval_jaxpr/jit(_where)/select_n | solution.py:60
  17.8 0.8 %bitcast_select_fusion.4 = s32[4,32]{1,0:T(4,128)S(1)} fusion(s32[8,4,1,32]{3,1,2,0:T(4,128)} %get-tuple-element.560, s32[]{:T(128)} %get-tuple-element.544, s32[]{:T(128)} %get-tuple-element.561, s32[4]{0:T(128)S(1)} %fusion.37), kind=kLoop, calls=%fused_computation.31.clone.1 | loop fusion | flops 384 | bytes 1048 | tf_op jit(solution)/shard_map/while/body/eval_jaxpr/jit(_where)/select_n | solution.py:60
  19.5 0.8 %bitcast_select_fusion.4 = s32[4,32]{1,0:T(4,128)S(1)} fusion(s32[8,4,1,32]{3,1,2,0:T(4,128)} %get-tuple-element.560, s32[]{:T(128)} %get-tuple-element.544, s32[]{:T(128)} %get-tuple-element.561, s32[4]{0:T(128)S(1)} %fusion.37), kind=kLoop, calls=%fused_computation.31.clone.1 | loop fusion | flops 384 | bytes 1048 | tf_op jit(solution)/shard_map/while/body/eval_jaxpr/jit(_where)/select_n | solution.py:60
  21.3 0.8 %bitcast_select_fusion.4 = s32[4,32]{1,0:T(4,128)S(1)} fusion(s32[8,4,1,32]{3,1,2,0:T(4,128)} %get-tuple-element.560, s32[]{:T(128)} %get-tuple-element.544, s32[]{:T(128)} %get-tuple-element.561, s32[4]{0:T(128)S(1)} %fusion.37), kind=kLoop, calls=%fused_computation.31.clone.1 | loop fusion | flops 384 | bytes 1048 | tf_op jit(solution)/shard_map/while/body/eval_jaxpr/jit(_where)/select_n | solution.py:60
  23.1 0.8 %bitcast_select_fusion.4 = s32[4,32]{1,0:T(4,128)S(1)} fusion(s32[8,4,1,32]{3,1,2,0:T(4,128)} %get-tuple-element.560, s32[]{:T(128)} %get-tuple-element.544, s32[]{:T(128)} %get-tuple-element.561, s32[4]{0:T(128)S(1)} %fusion.37), kind=kLoop, calls=%fused_computation.31.clone.1 | loop fusion | flops 384 | bytes 1048 | tf_op jit(solution)/shard_map/while/body/eval_jaxpr/jit(_where)/select_n | solution.py:60
  24.9 0.8 %bitcast_select_fusion.4 = s32[4,32]{1,0:T(4,128)S(1)} fusion(s32[8,4,1,32]{3,1,2,0:T(4,128)} %get-tuple-element.560, s32[]{:T(128)} %get-tuple-element.544, s32[]{:T(128)} %get-tuple-element.561, s32[4]{0:T(128)S(1)} %fusion.37), kind=kLoop, calls=%fused_computation.31.clone.1 | loop fusion | flops 384 | bytes 1048 | tf_op jit(solution)/shard_map/while/body/eval_jaxpr/jit(_where)/select_n | solution.py:60
  26.7 0.8 %bitcast_select_fusion.4 = s32[4,32]{1,0:T(4,128)S(1)} fusion(s32[8,4,1,32]{3,1,2,0:T(4,128)} %get-tuple-element.560, s32[]{:T(128)} %get-tuple-element.544, s32[]{:T(128)} %get-tuple-element.561, s32[4]{0:T(128)S(1)} %fusion.37), kind=kLoop, calls=%fused_computation.31.clone.1 | loop fusion | flops 384 | bytes 1048 | tf_op jit(solution)/shard_map/while/body/eval_jaxpr/jit(_where)/select_n | solution.py:60
  28.4 8.5 %all-gather.2 = f32[32,4,1,256]{3,1,2,0:T(4,128)S(1)} all-gather(f32[8,4,1,256]{3,1,2,0:T(4,128)S(1)} %get-tuple-element.250), channel_id=4, replica_groups=mesh['tbl'=8,'grp'=4] {'grp'}, dimensions={0}, use_global_device_ids=true | all-gather | bytes 163840 | tf_op jit(solution)/shard_map/all_gather | solution.py:8
  37.0 7.2 %all-gather = f32[32,4,1]{1,2,0:T(1,128)S(1)} all-gather(f32[8,4,1]{1,2,0:T(1,128)S(1)} %get-tuple-element.248), channel_id=2, replica_groups=mesh['tbl'=8,'grp'=4] {'grp'}, dimensions={0}, use_global_device_ids=true | all-gather | bytes 640 | tf_op jit(solution)/shard_map/all_gather | solution.py:8
  44.3 8.2 %all-gather.1 = f32[32,4,1]{1,2,0:T(1,128)S(1)} all-gather(f32[8,4,1]{1,2,0:T(1,128)S(1)} %get-tuple-element.249), channel_id=3, replica_groups=mesh['tbl'=8,'grp'=4] {'grp'}, dimensions={0}, use_global_device_ids=true | all-gather | bytes 640 | tf_op jit(solution)/shard_map/all_gather | solution.py:8
  52.7 1.4 %while.34 = (s32[]{:T(128)}, f32[8,4,1,1]{0,1,3,2:T(4,128)S(1)}, f32[8,4,1,1]{0,1,3,2:T(4,128)S(1)}, f32[8,4,1,1,256]{4,3,2,1,0:T(1,128)S(1)}, f32[4,8,4,1,1]{1,...) while((s32[]{:T(128)}, f32[8,4,1,1]{0,1,3,2:T(4,128)S(1)}, ...), condition=%wide.region_8.9_spmd, body=%wide.region_7.8_spmd.sunk | while | flops 24805 | bytes 166427 | solution.py:14
  54.7 0.7 reduce.6
  56.0 4.9 %all-to-all-start = ((bf16[8,2,128]{2,1,0:T(2,128)(2,1)}), bf16[8,2,128]{2,1,0:T(2,128)(2,1)S(1)}, u32[]{:S(2)}, u32[]{:S(2)}) async-start(bf16[8,2,128]{2,1,0:T(2,128)(2,1)} %reshape.352), calls=%async_computation | async-start | bytes 8192 | tf_op jit(solution)/shard_map/all_to_all | solution.py:98
  60.9 0.6 copy-done.4
  61.5 1.0 %sort.17 = (s32[8]{0:T(128)}, s32[8]{0:T(128)S(1)}) sort(s32[8]{0:T(128)S(1)} %copy-done.4, s32[8]{0:T(128)S(1)} %iota.10), dimensions={0}, to_apply=%region_0.1 | sort | flops 24 | bytes 128 | tf_op jit(solution)/shard_map/jit(argsort)/sort | solution.py:100
  62.6 3.8 %all-to-all-done = bf16[8,2,128]{2,1,0:T(2,128)(2,1)S(1)} async-done(((bf16[8,2,128]{2,1,0:T(2,128)(2,1)}), bf16[8,2,128]{2,1,0:T(2,128)(2,1)S(1)}, u32[]{:S(2)}, u32[]{:S(2)}) %all-to-all-start) | async-done | bytes 4128 | tf_op jit(solution)/shard_map/all_to_all | solution.py:98
  67.0 0.7 bitcast_select_fusion.2
  (116 shorter events, 13.1 us)
Async XLA Ops:
  0.0 0.7 copy-start.2
  0.7 0.7 %copy-start = (f32[1,256]{1,0:T(1,128)S(1)}, f32[1,256]{1,0:T(1,128)}, u32[]{:S(2)}) copy-start(f32[1,256]{1,0:T(1,128)} %param.11) | copy-start | bytes 3076
  1.4 0.9 %copy-start.1 = (bf16[1,256,256]{2,1,0:T(8,128)(2,1)S(1)}, bf16[1,256,256]{2,1,0:T(8,128)(2,1)}, u32[]{:S(2)}) copy-start(bf16[1,256,256]{2,1,0:T(8,128)(2,1)} %param.10) | copy-start | bytes 393220
  12.8 0.7 copy-start.3
  56.0 10.4 %all-to-all-start = ((bf16[8,2,128]{2,1,0:T(2,128)(2,1)}), bf16[8,2,128]{2,1,0:T(2,128)(2,1)S(1)}, u32[]{:S(2)}, u32[]{:S(2)}) async-start(bf16[8,2,128]{2,1,0:T(2,128)(2,1)} %reshape.352), calls=%async_computation | async-start | bytes 8192 | tf_op jit(solution)/shard_map/all_to_all | solution.py:98
  60.9 0.7 copy-start.4
